TPU v7x, 32 devices: a whole 2x2x4 slice. The times are simulated.
32 devices in a mesh: dp: 8 (over z, y), mp: 4 (over x, core).
Axes of the slice: x: 2, y: 2, z: 4, core: 2. Of those that a mesh axis runs over, the one named last changes fastest.
Arguments:
- tokens: bfloat16 [8192, 2048], P('dp'), may hold values from -6 to 6
- out_cot: bfloat16 [8192, 2048], P('dp'), may hold values from -23 to 23
- lengths: int32 [8], P('dp'), may hold values from 1 to 1024, 6144 in all
- seq_family: int32 [8, 1], P('dp'), may hold values from 0 to 3
- family_tokens: int32 [4], replicated, may hold values from 100000 to 3999999
- norm_master: float32 [2048, 6], P('dp'), may hold values from -0.5 to 2.4, as said below
- attn_bias_master: float32 [2, 2048], P(None, 'mp'), may hold values from -2 to 2
- qkv_master: float32 [2048, 3, 2048], P('dp', None, 'mp'), may hold values from -0.125 to 0.125
- proj_master: float32 [2048, 2048], P('dp', 'mp'), may hold values from -1.5 to 1.5
- fc_bias_master: float32 [8192], P('mp'), may hold values from -1.5 to 1.5
- fc_master: float32 [2048, 8192], P('dp', 'mp'), may hold values from -0.125 to 0.125
- down_master: float32 [2048, 8192], P('dp', 'mp'), may hold values from -0.0625 to 0.0625
- norm_moment: float32 [2048, 6], P('dp'), may hold values from -0.0008544922 to 0.0008544922
- attn_bias_moment: float32 [2, 2048], P(None, 'mp'), may hold values from -0.0008544922 to 0.0008544922
- qkv_moment: float32 [2048, 3, 2048], P('dp', None, 'mp'), may hold values from -0.0008544922 to 0.0008544922
- proj_moment: float32 [2048, 2048], P('dp', 'mp'), may hold values from -0.0008544922 to 0.0008544922
- fc_bias_moment: float32 [8192], P('mp'), may hold values from -0.0008544922 to 0.0008544922
- fc_moment: float32 [2048, 8192], P('dp', 'mp'), may hold values from -0.0008544922 to 0.0008544922
- down_moment: float32 [2048, 8192], P('dp', 'mp'), may hold values from -0.0008544922 to 0.0008544922
- norm_average: float32 [2048, 6], P('dp'), may hold values from 0.5 to 1.5
- attn_bias_average: float32 [2, 2048], P(None, 'mp'), may hold values from -2 to 2
- qkv_average: float32 [2048, 3, 2048], P('dp', None, 'mp'), may hold values from -0.125 to 0.125
- proj_average: float32 [2048, 2048], P('dp', 'mp'), may hold values from -1.5 to 1.5
- fc_bias_average: float32 [8192], P('mp'), may hold values from -1.5 to 1.5
- fc_average: float32 [2048, 8192], P('dp', 'mp'), may hold values from -0.125 to 0.125
- down_average: float32 [2048, 8192], P('dp', 'mp'), may hold values from -0.0625 to 0.0625
Outputs:
- block_out: bfloat16 [8192, 2048], P('dp')
- input_grad: float32 [8192, 2048], P('dp')
- norm_grad: float32 [2048, 6], P('dp')
- attn_bias_grad: float32 [2, 2048], P(None, 'mp')
- qkv_grad: float32 [2048, 3, 2048], P('dp', None, 'mp')
- proj_grad: float32 [2048, 2048], P('dp', 'mp')
- fc_bias_grad: float32 [8192], P('mp')
- fc_grad: float32 [2048, 8192], P('dp', 'mp')
- down_grad: float32 [2048, 8192], P('dp', 'mp')
- norm_momentum: float32 [2048, 6], P('dp')
- attn_bias_momentum: float32 [2, 2048], P(None, 'mp')
- qkv_momentum: float32 [2048, 3, 2048], P('dp', None, 'mp')
- proj_momentum: float32 [2048, 2048], P('dp', 'mp')
- fc_bias_momentum: float32 [8192], P('mp')
- fc_momentum: float32 [2048, 8192], P('dp', 'mp')
- down_momentum: float32 [2048, 8192], P('dp', 'mp')
- norm_averaged: float32 [2048, 6], P('dp')
- attn_bias_averaged: float32 [2, 2048], P(None, 'mp')
- qkv_averaged: float32 [2048, 3, 2048], P('dp', None, 'mp')
- proj_averaged: float32 [2048, 2048], P('dp', 'mp')
- fc_bias_averaged: float32 [8192], P('mp')
- fc_averaged: float32 [2048, 8192], P('dp', 'mp')
- down_averaged: float32 [2048, 8192], P('dp', 'mp')
- norm_updated: float32 [2048, 6], P('dp')
- attn_bias_updated: float32 [2, 2048], P(None, 'mp')
- qkv_updated: float32 [2048, 3, 2048], P('dp', None, 'mp')
- proj_updated: float32 [2048, 2048], P('dp', 'mp')
- fc_bias_updated: float32 [8192], P('mp')
- fc_updated: float32 [2048, 8192], P('dp', 'mp')
- down_updated: float32 [2048, 8192], P('dp', 'mp')
- norm_copy: bfloat16 [2048, 6], P('dp')
- attn_bias_copy: bfloat16 [2, 2048], P(None, 'mp')
- qkv_copy: bfloat16 [2048, 3, 2048], P('dp', None, 'mp')
- proj_copy: bfloat16 [2048, 2048], P('dp', 'mp')
- fc_bias_copy: bfloat16 [8192], P('mp')
- fc_copy: bfloat16 [2048, 8192], P('dp', 'mp')
- down_copy: bfloat16 [2048, 8192], P('dp', 'mp')
- grad_norm: float32 [], replicated
Inputs may be any that keep to these rules, and one draw needn't show every extreme that they name: `lengths`: they sum to 6144; the longest is 1024. `seq_family`: every family has a sequence. `norm_master`: gains positive, biases of either sign.
All inputs are finite; a program needn't handle non-finite values. No bound on the sum of `lengths` on one device may be relied on, other than what follows from the above.
Results may differ from a plain program's by a relative error of at most 0.012.
The roundings to bfloat16 on the way count: a program that leaves them out, or rounds other values in their place, can miss the bound.
Values may be sent and summed in bfloat16 or wider, within the bound.
A program may use at most 256 MiB of HBM per device.

v0:
```python
import math
import jax
import jax.numpy as jnp
from jax import lax
from jax.sharding import PartitionSpec as P

HEAD_DIM = 128
LEN = 1024
EPS = 1e-05
MOMENTUM = 0.9
RATE = 192.0
KEEP = 0.9
NEG = -1e30


def layer_norm(value, gain, shift):
    centre = jnp.mean(value, axis=-1, keepdims=True)
    centred = value - centre
    spread = jnp.mean(centred * centred, axis=-1, keepdims=True)
    return centred * lax.rsqrt(spread + EPS) * gain + shift


def gelu_tanh(value):
    return (
        0.5
        * value
        * (1.0 + jnp.tanh(0.7978845608028654 * (value + 0.044715 * value * value * value)))
    )


def local(
    tokens,
    out_cot,
    lengths,
    seq_family,
    family_tokens,
    norm_master,
    attn_bias_master,
    qkv_master,
    proj_master,
    fc_bias_master,
    fc_master,
    down_master,
    norm_moment,
    attn_bias_moment,
    qkv_moment,
    proj_moment,
    fc_bias_moment,
    fc_moment,
    down_moment,
    norm_average,
    attn_bias_average,
    qkv_average,
    proj_average,
    fc_bias_average,
    fc_average,
    down_average,
):
    seq_count = lengths.shape[0]
    row_count = tokens.shape[0]
    seq_len = row_count // seq_count
    family_count = family_tokens.shape[0]
    local_heads = qkv_master.shape[2] // HEAD_DIM
    head_width = qkv_master.shape[2]
    scale = 1.0 / math.sqrt(HEAD_DIM)
    mp_count = lax.axis_size("mp")
    dp_count = lax.axis_size("dp")

    def sum_over_mp(term_fn):
        summed = lax.psum(term_fn(0, row_count), "mp")
        return summed

    family_ids = jnp.arange(family_count, dtype=jnp.int32)
    member = seq_family == family_ids[None, :]
    local_counts = jnp.sum(jnp.where(member, lengths[:, None], 0), axis=0).astype(jnp.float32)
    counts = lax.psum(local_counts, "dp")
    valid_total = jnp.sum(counts)
    share = family_tokens.astype(jnp.float32) / jnp.sum(family_tokens).astype(jnp.float32)
    family_weight = share * valid_total / jnp.maximum(counts, float(LEN // 2))
    seq_weight = jnp.sum(jnp.where(member, family_weight[None, :], 0.0), axis=1)
    places = jnp.arange(seq_len, dtype=jnp.int32)
    token_weight = jnp.where(places[None, :] < lengths[:, None], seq_weight[:, None], 0.0).reshape(
        row_count
    )
    causal = places[:, None] >= places[None, :]
    low_norm = norm_master.astype(jnp.bfloat16)
    low_qkv = qkv_master.astype(jnp.bfloat16)
    low_proj = proj_master.astype(jnp.bfloat16)
    low_fc = fc_master.astype(jnp.bfloat16)
    low_down = down_master.astype(jnp.bfloat16)
    w_qkv, w_proj, w_fc, w_down, w_norm = (
        lax.all_gather(low_qkv, "dp", axis=0, tiled=True),
        lax.all_gather(low_proj, "dp", axis=0, tiled=True),
        lax.all_gather(low_fc, "dp", axis=0, tiled=True),
        lax.all_gather(low_down, "dp", axis=0, tiled=True),
        lax.all_gather(low_norm, "dp", axis=0, tiled=True),
    )
    norm_full = w_norm.astype(jnp.float32)
    bias_rows = jnp.stack(
        [attn_bias_master[0], jnp.zeros_like(attn_bias_master[0]), attn_bias_master[1]], axis=0
    )
    x_in = tokens.astype(jnp.float32)
    ln1_low = layer_norm(x_in, norm_full[:, 0], norm_full[:, 1]).astype(jnp.bfloat16)
    qkv = (
        jnp.einsum("td,dce->tce", ln1_low, w_qkv, preferred_element_type=jnp.float32)
        + bias_rows[None]
    )
    qkv = qkv.astype(jnp.bfloat16)
    heads = qkv.reshape(seq_count, seq_len, 3, local_heads, HEAD_DIM)

    def attend(one_seq):
        query_rows = one_seq[:, 0]
        key_rows = one_seq[:, 1]
        value_rows = one_seq[:, 2]
        scores = (
            jnp.einsum("qhd,khd->hqk", query_rows, key_rows, preferred_element_type=jnp.float32)
            * scale
        )
        scores = jnp.where(causal[None], scores, NEG)
        row_top = jnp.max(scores, axis=-1, keepdims=True)
        log_total = row_top + jnp.log(jnp.sum(jnp.exp(scores - row_top), axis=-1, keepdims=True))
        attn_prob = jnp.exp(scores - log_total).astype(jnp.bfloat16)
        mixed = jnp.einsum(
            "hqk,khd->qhd", attn_prob, value_rows, preferred_element_type=jnp.float32
        )
        return (mixed.astype(jnp.bfloat16), log_total)

    mixed_low, log_kept = lax.map(attend, heads)
    mixed_low = mixed_low.reshape(row_count, head_width)

    def attn_term(start, count):
        return jnp.einsum("te,de->td", mixed_low, w_proj, preferred_element_type=jnp.float32)

    residual_part = x_in + sum_over_mp(attn_term) + norm_full[:, 4]
    ln2_part, ln2_back = jax.vjp(layer_norm, residual_part, norm_full[:, 2], norm_full[:, 3])
    ln2_low = ln2_part.astype(jnp.bfloat16)
    pre_act = (
        jnp.einsum("td,df->tf", ln2_low, w_fc, preferred_element_type=jnp.float32)
        + fc_bias_master[None]
    )
    hidden_act, gelu_back = jax.vjp(gelu_tanh, pre_act)
    hidden_low = hidden_act.astype(jnp.bfloat16)

    def mlp_term(start, count):
        return jnp.einsum("tf,df->td", hidden_low, w_down, preferred_element_type=jnp.float32)

    block_part = (residual_part + sum_over_mp(mlp_term) + norm_full[:, 5]).astype(jnp.bfloat16)
    upstream = token_weight[:, None] * out_cot.astype(jnp.float32)
    upstream_low = upstream.astype(jnp.bfloat16)
    down_sum = jnp.einsum("td,tf->df", upstream_low, hidden_low, preferred_element_type=jnp.float32)
    back_act = jnp.einsum("td,df->tf", upstream_low, w_down, preferred_element_type=jnp.float32)
    back_pre = gelu_back(back_act)[0].astype(jnp.bfloat16)
    fc_bias_sum = jnp.sum(back_pre, axis=0, dtype=jnp.float32)
    fc_sum = jnp.einsum("td,tf->df", ln2_low, back_pre, preferred_element_type=jnp.float32)

    def fc_back_term(start, count):
        return jnp.einsum("tf,df->td", back_pre, w_fc, preferred_element_type=jnp.float32)

    back_ln2 = sum_over_mp(fc_back_term)
    back_resid_part, gain2_sum, shift2_sum = ln2_back(back_ln2)
    back_resid_part = upstream + back_resid_part
    back_attn_low = back_resid_part.astype(jnp.bfloat16)
    proj_sum = jnp.einsum("td,te->de", back_attn_low, mixed_low, preferred_element_type=jnp.float32)
    back_mixed = jnp.einsum(
        "td,de->te", back_attn_low, w_proj, preferred_element_type=jnp.float32
    ).astype(jnp.bfloat16)
    back_mixed = back_mixed.reshape(seq_count, seq_len, local_heads, HEAD_DIM)

    def attend_back(items):
        one_seq, log_total, back_seq = items
        query_rows = one_seq[:, 0]
        key_rows = one_seq[:, 1]
        value_rows = one_seq[:, 2]
        scores = (
            jnp.einsum("qhd,khd->hqk", query_rows, key_rows, preferred_element_type=jnp.float32)
            * scale
        )
        scores = jnp.where(causal[None], scores, NEG)
        attn_prob = jnp.exp(scores - log_total)
        prob_low = attn_prob.astype(jnp.bfloat16)
        back_value = jnp.einsum(
            "hqk,qhd->khd", prob_low, back_seq, preferred_element_type=jnp.float32
        )
        back_prob = jnp.einsum(
            "qhd,khd->hqk", back_seq, value_rows, preferred_element_type=jnp.float32
        )
        back_score = attn_prob * (
            back_prob - jnp.sum(attn_prob * back_prob, axis=-1, keepdims=True)
        )
        back_score = back_score.astype(jnp.bfloat16)
        back_query = (
            jnp.einsum("hqk,khd->qhd", back_score, key_rows, preferred_element_type=jnp.float32)
            * scale
        )
        back_key = (
            jnp.einsum("hqk,qhd->khd", back_score, query_rows, preferred_element_type=jnp.float32)
            * scale
        )
        return jnp.stack([back_query, back_key, back_value], axis=1).astype(jnp.bfloat16)

    back_heads = lax.map(attend_back, (heads, log_kept, back_mixed))
    back_qkv = back_heads.reshape(row_count, 3, head_width)
    attn_bias_sum = jnp.sum(back_qkv[:, 0::2], axis=0, dtype=jnp.float32)
    qkv_sum = jnp.einsum("td,tce->dce", ln1_low, back_qkv, preferred_element_type=jnp.float32)

    def qkv_back_term(start, count):
        return jnp.einsum("tce,dce->td", back_qkv, w_qkv, preferred_element_type=jnp.float32)

    back_ln1 = sum_over_mp(qkv_back_term)
    ln1_again, ln1_back = jax.vjp(layer_norm, x_in, norm_full[:, 0], norm_full[:, 1])
    back_input, gain1_sum, shift1_sum = ln1_back(back_ln1)
    whole = back_resid_part + back_input
    norm_part = jnp.stack(
        [
            gain1_sum,
            shift1_sum,
            gain2_sum,
            shift2_sum,
            jnp.sum(back_resid_part, axis=0),
            jnp.sum(upstream, axis=0),
        ],
        axis=1,
    )
    qkv_reduced, proj_reduced, fc_reduced, down_reduced, norm_reduced = (
        lax.psum_scatter(qkv_sum, "dp", scatter_dimension=0, tiled=True),
        lax.psum_scatter(proj_sum, "dp", scatter_dimension=0, tiled=True),
        lax.psum_scatter(fc_sum, "dp", scatter_dimension=0, tiled=True),
        lax.psum_scatter(down_sum, "dp", scatter_dimension=0, tiled=True),
        lax.psum_scatter(norm_part, "dp", scatter_dimension=0, tiled=True),
    )
    attn_bias_reduced, fc_bias_reduced = lax.psum((attn_bias_sum, fc_bias_sum), "dp")
    raw_grads = [
        reduced / valid_total
        for reduced in (
            norm_reduced,
            attn_bias_reduced,
            qkv_reduced,
            proj_reduced,
            fc_bias_reduced,
            fc_reduced,
            down_reduced,
        )
    ]
    local_squares = jnp.sum(raw_grads[0] * raw_grads[0]) / float(mp_count)
    local_squares = local_squares + jnp.sum(raw_grads[1] * raw_grads[1]) / float(dp_count)
    local_squares = local_squares + jnp.sum(raw_grads[4] * raw_grads[4]) / float(dp_count)
    for grad_raw in (raw_grads[2], raw_grads[3], raw_grads[5], raw_grads[6]):
        local_squares = local_squares + jnp.sum(grad_raw * grad_raw)
    squares = lax.psum(local_squares, ("dp", "mp"))
    grad_norm = jnp.sqrt(squares)
    clip_factor = jnp.minimum(1.0, 1.0 / (grad_norm + 1e-06))
    masters = (
        norm_master,
        attn_bias_master,
        qkv_master,
        proj_master,
        fc_bias_master,
        fc_master,
        down_master,
    )
    moments = (
        norm_moment,
        attn_bias_moment,
        qkv_moment,
        proj_moment,
        fc_bias_moment,
        fc_moment,
        down_moment,
    )
    averages = (
        norm_average,
        attn_bias_average,
        qkv_average,
        proj_average,
        fc_bias_average,
        fc_average,
        down_average,
    )
    grads_out = []
    momenta_out = []
    averaged_out = []
    updated_out = []
    copies_out = []
    for master, moment, average, grad_raw in zip(masters, moments, averages, raw_grads):
        clipped = grad_raw * clip_factor
        momentum = MOMENTUM * moment + clipped
        updated = master - RATE * (clipped + MOMENTUM * momentum)
        averaged = KEEP * average + (1.0 - KEEP) * updated
        grads_out.append(clipped)
        momenta_out.append(momentum)
        averaged_out.append(averaged)
        updated_out.append(updated)
        copies_out.append(updated.astype(jnp.bfloat16))
    return (
        block_part,
        whole,
        grads_out[0],
        grads_out[1],
        grads_out[2],
        grads_out[3],
        grads_out[4],
        grads_out[5],
        grads_out[6],
        momenta_out[0],
        momenta_out[1],
        momenta_out[2],
        momenta_out[3],
        momenta_out[4],
        momenta_out[5],
        momenta_out[6],
        averaged_out[0],
        averaged_out[1],
        averaged_out[2],
        averaged_out[3],
        averaged_out[4],
        averaged_out[5],
        averaged_out[6],
        updated_out[0],
        updated_out[1],
        updated_out[2],
        updated_out[3],
        updated_out[4],
        updated_out[5],
        updated_out[6],
        copies_out[0],
        copies_out[1],
        copies_out[2],
        copies_out[3],
        copies_out[4],
        copies_out[5],
        copies_out[6],
        grad_norm,
    )


def solution(mesh):
    placed = (
        P("dp", None),
        P("dp", None),
        P("dp"),
        P("dp", None),
        P(),
        P("dp", None),
        P(None, "mp"),
        P("dp", None, "mp"),
        P("dp", "mp"),
        P("mp"),
        P("dp", "mp"),
        P("dp", "mp"),
        P("dp", None),
        P(None, "mp"),
        P("dp", None, "mp"),
        P("dp", "mp"),
        P("mp"),
        P("dp", "mp"),
        P("dp", "mp"),
        P("dp", None),
        P(None, "mp"),
        P("dp", None, "mp"),
        P("dp", "mp"),
        P("mp"),
        P("dp", "mp"),
        P("dp", "mp"),
    )
    return jax.shard_map(
        local,
        mesh=mesh,
        in_specs=placed,
        out_specs=(
            P("dp", None),
            P("dp", None),
            P("dp", None),
            P(None, "mp"),
            P("dp", None, "mp"),
            P("dp", "mp"),
            P("mp"),
            P("dp", "mp"),
            P("dp", "mp"),
            P("dp", None),
            P(None, "mp"),
            P("dp", None, "mp"),
            P("dp", "mp"),
            P("mp"),
            P("dp", "mp"),
            P("dp", "mp"),
            P("dp", None),
            P(None, "mp"),
            P("dp", None, "mp"),
            P("dp", "mp"),
            P("mp"),
            P("dp", "mp"),
            P("dp", "mp"),
            P("dp", None),
            P(None, "mp"),
            P("dp", None, "mp"),
            P("dp", "mp"),
            P("mp"),
            P("dp", "mp"),
            P("dp", "mp"),
            P("dp", None),
            P(None, "mp"),
            P("dp", None, "mp"),
            P("dp", "mp"),
            P("mp"),
            P("dp", "mp"),
            P("dp", "mp"),
            P(),
        ),
        check_vma=False,
    )
```

profile of v0, /device:TPU:0, one launch (start us, length us, event | category | flops | bytes accessed | tf_op | source)
XLA Modules:
  0.0 2152.3 jit_solution(12280135592228971859)
XLA Ops:
  15.6 3.4 fusion.15
  19.1 32.9 %all_gather.15 = bf16[2048,6]{0,1:T(8,128)(2,1)S(1)} all-gather(bf16[256,6]{0,1:T(8,128)(2,1)S(1)} %convert_element_type.108), channel_id=1, replica_groups=mesh['dp'=8,'mp'=4] {'dp'}, dimensions={0}, use_global_device_ids=true | all-gather | bytes 27648 | tf_op jit(solution)/shard_map/all_gather | solution.py:96
  52.7 61.0 %all-gather.5.cloned.1.call-done = bf16[2048,3,512]{0,2,1:T(8,128)(2,1)} async-done(((bf16[256,3,512]{0,2,1:T(8,128)(2,1)}), bf16[2048,3,512]{0,2,1:T(8,128)(2,1)}) %all-gather.5.cloned.1.call-update) | async-done | bytes 6291472 | tf_op jit(solution)/shard_map/all_gather | solution.py:92
  113.7 11.1 add_convert_fusion.2
  124.9 3.3 fusion
  128.3 3.7 exponential_reduce_fusion
  134.0 6.5 convolution_convert_fusion.1
  140.5 23.5 %all-gather.7.cloned.1.call-done = bf16[2048,512]{1,0:T(8,128)(2,1)} async-done(((bf16[256,512]{1,0:T(8,128)(2,1)}), bf16[2048,512]{1,0:T(8,128)(2,1)}) %all-gather.7.cloned.1.call-update) | async-done | bytes 2097168 | tf_op jit(solution)/shard_map/all_gather | solution.py:93
  164.0 7.4 fusion.66
  174.3 3.2 convert_element_type.120
  178.8 18.5 psum.58
  201.1 121.8 %all-reduce.6.cloned.1.call-done = f32[1024,2048]{1,0:T(8,128)} async-done(((f32[1024,2048]{1,0:T(8,128)}), f32[1024,2048]{1,0:T(8,128)}) %all-reduce.6.cloned.1.call-update) | async-done | bytes 8388624 | tf_op jit(solution)/shard_map/psum | solution.py:70
  322.9 5.8 fusion.62
  328.7 3.3 copy-done
  333.0 117.6 %all-gather.9.cloned.1.call-done = bf16[2048,2048]{1,0:T(8,128)(2,1)} async-done(((bf16[256,2048]{1,0:T(8,128)(2,1)}), bf16[2048,2048]{1,0:T(8,128)(2,1)}) %all-gather.9.cloned.1.call-update) | async-done | bytes 8388624 | tf_op jit(solution)/shard_map/all_gather | solution.py:94
  450.6 15.9 fusion.51
  466.5 109.8 %all-gather.11.cloned.1.call-done = bf16[2048,2048]{1,0:T(8,128)(2,1)} async-done(((bf16[256,2048]{1,0:T(8,128)(2,1)}), bf16[2048,2048]{1,0:T(8,128)(2,1)}) %all-gather.11.cloned.1.call-update) | async-done | bytes 8388624 | tf_op jit(solution)/shard_map/all_gather | solution.py:95
  576.3 21.0 convert_reduce_fusion.1
  599.2 11.1 fusion.67
  610.3 18.3 fusion.49
  628.6 132.9 %all-reduce.8.cloned.1.call-done = f32[1024,2048]{1,0:T(8,128)} async-done(((f32[1024,2048]{1,0:T(8,128)}), f32[1024,2048]{1,0:T(8,128)}) %all-reduce.8.cloned.1.call-update) | async-done | bytes 8388624 | tf_op jit(solution)/shard_map/psum | solution.py:70
  761.5 7.5 multiply_reduce_fusion.1
  769.7 5.0 fusion.61
  774.7 6.3 fusion.33
  781.1 9.7 convolution_convert_fusion
  790.7 12.6 multiply_reduce_fusion
  803.3 12.1 multiply_convert_fusion
  823.1 11.0 convolution_bitcast_fusion
  835.3 9.5 fusion.23
  844.9 278.3 %all-reduce.10.cloned.1.call-done = (f32[1024,2048]{1,0:T(8,128)}, f32[1024,2048]{1,0:T(8,128)}) async-done(((f32[1024,2048]{1,0:T(8,128)}, f32[1024,2048]{1,0:T(8,128)}), (f32[1024,2048]{1,0:T(8,128)}, f32[1024,2048]{1,0:T(8,128)})) %all-reduce.10.cloned.1.call-update) | async-done | bytes 16777232 | tf_op jit(solution)/shard_map/psum | solution.py:70
  1123.3 6.4 fusion.53
  1131.6 3.9 fusion.10
  1135.5 10.2 fusion.20
  1146.7 13.6 fusion.36
  1161.0 16.4 fusion.50
  1177.7 17.1 fusion.27
  1195.5 37.8 %all-reduce = (f32[2,512]{1,0:T(2,128)S(1)}, f32[2048]{0:T(1024)S(1)}) all-reduce(f32[2,512]{1,0:T(2,128)S(1)} %convert_reduce_fusion.2, f32[2048]{0:T(1024)S(1)} %copy-done.48), channel_id=1, replica_groups=mesh['dp'=8,'mp'=4] {'dp'}, use_global_device_ids=true, to_apply=%region_28.29 | all-reduce | flops 3072 | bytes 24576 | tf_op jit(solution)/shard_map/psum | solution.py:231
  1239.6 41.7 %reduce-scatter.6.cloned.1.call-done = f32[256,6]{0,1:T(8,128)} async-done(((f32[2048,6]{0,1:T(8,128)}), f32[256,6]{0,1:T(8,128)}) %reduce-scatter.6.cloned.1.call-update) | async-done | bytes 6160 | tf_op jit(solution)/shard_map/reduce_scatter | solution.py:229
  1283.9 208.1 %reduce-scatter.8.cloned.1.call-done = f32[256,3,512]{2,0,1:T(8,128)} async-done(((f32[2048,3,512]{2,0,1:T(8,128)}), f32[256,3,512]{2,0,1:T(8,128)}) %reduce-scatter.8.cloned.1.call-update) | async-done | bytes 1572880 | tf_op jit(solution)/shard_map/reduce_scatter | solution.py:225
  1496.3 280.9 %reduce-scatter.12.cloned.1.call-done = f32[256,2048]{1,0:T(8,128)} async-done(((f32[2048,2048]{1,0:T(8,128)}), f32[256,2048]{1,0:T(8,128)}) %reduce-scatter.12.cloned.1.call-update) | async-done | bytes 2097168 | tf_op jit(solution)/shard_map/reduce_scatter | solution.py:227
  1777.2 3.4 multiply_reduce_fusion.5
  1781.3 281.4 %reduce-scatter.14.cloned.1.call-done = f32[256,2048]{1,0:T(8,128)} async-done(((f32[2048,2048]{1,0:T(8,128)}), f32[256,2048]{1,0:T(8,128)}) %reduce-scatter.14.cloned.1.call-update) | async-done | bytes 2097168 | tf_op jit(solution)/shard_map/reduce_scatter | solution.py:228
  2062.7 3.4 multiply_reduce_fusion.4
  2066.9 10.2 add_convert_fusion
  2077.0 39.2 %psum.63 = f32[]{:T(128)} all-reduce(f32[]{:T(128)S(6)} %add.249), channel_id=1, replica_groups=mesh['dp'=8,'mp'=4] {'dp','mp'}, use_global_device_ids=true, to_apply=%region_41.42 | all-reduce | flops 1 | bytes 8 | tf_op jit(solution)/shard_map/psum | solution.py:249
  2122.0 3.2 fusion.57
  2127.5 5.9 fusion.58
  2135.1 5.1 fusion.54
  (190 shorter events, 57.0 us)
Async XLA Ops:
  7.2 11.8 copy-start.40
  7.2 106.5 %all-gather.5.cloned.1.call-start = ((), (), s32[]{:S(2)}) async-start(), calls=%async_computation.5 | async-start | bytes 7077888 | tf_op jit(solution)/shard_map/all_gather | solution.py:92
  9.9 154.1 %all-gather.7.cloned.1.call-start = ((), (), s32[]{:S(2)}) async-start(), calls=%async_computation.6 | async-start | bytes 2359296 | tf_op jit(solution)/shard_map/all_gather | solution.py:93
  11.7 311.2 %all-reduce.6.cloned.1.call-start = ((), (), s32[]{:S(2)}) async-start(), calls=%async_computation.7 | async-start | bytes 16777216 | tf_op jit(solution)/shard_map/psum | solution.py:70
  15.6 109.2 %copy-start.28 = (f32[1024]{0:T(1024)}, f32[1024]{0:T(1024)S(1)}, u32[]{:S(2)}) copy-start(f32[1024]{0:T(1024)S(1)} %broadcast_multiply_fusion.8) | copy-start | bytes 12292
  19.0 105.8 %copy-start.32 = (f32[1024]{0:T(1024)}, f32[1024]{0:T(1024)S(1)}, u32[]{:S(2)}) copy-start(f32[1024]{0:T(1024)S(1)} %fusion.15) | copy-start | bytes 12292
  19.1 105.8 %copy-start.30 = (f32[1024]{0:T(1024)}, f32[1024]{0:T(1024)S(1)}, u32[]{:S(2)}) copy-start(f32[1024]{0:T(1024)S(1)} %fusion.42) | copy-start | bytes 12292
  52.6 72.3 %copy-start.26 = (f32[2048,1]{0,1:T(1,128)}, f32[2048,1]{0,1:T(1,128)S(1)}, u32[]{:S(2)}) copy-start(f32[2048,1]{0,1:T(1,128)S(1)} %get-tuple-element.123) | copy-start | bytes 24580
  52.6 72.3 %copy-start.46 = (f32[2048,1]{0,1:T(1,128)}, f32[2048,1]{0,1:T(1,128)S(1)}, u32[]{:S(2)}) copy-start(f32[2048,1]{0,1:T(1,128)S(1)} %get-tuple-element.124) | copy-start | bytes 24580
  52.6 398.0 %copy-start.44 = (f32[2048,1]{0,1:T(1,128)}, f32[2048,1]{0,1:T(1,128)S(1)}, u32[]{:S(2)}) copy-start(f32[2048,1]{0,1:T(1,128)S(1)} %get-tuple-element.121) | copy-start | bytes 24580
  140.4 31.0 %copy-start.56 = (bf16[4,128,1024]{2,1,0:T(8,128)(2,1)}, bf16[4,128,1024]{2,1,0:T(8,128)(2,1)S(1)}, u32[]{:S(2)}) copy-start(bf16[4,128,1024]{2,1,0:T(8,128)(2,1)S(1)} %convolution_convert_fusion.1) | copy-start | bytes 3145732
  171.4 25.9 %copy-start.54 = (s32[4]{0:T(128)S(1)}, s32[4]{0:T(128)}, u32[]{:S(2)}) copy-start(s32[4]{0:T(128)} %param.30) | copy-start | bytes 52
  171.4 279.2 %all-gather.9.cloned.1.call-start = ((), (), s32[]{:S(2)}) async-start(), calls=%async_computation.8 | async-start | bytes 9437184 | tf_op jit(solution)/shard_map/all_gather | solution.py:94
  174.2 402.1 %all-gather.11.cloned.1.call-start = ((), (), s32[]{:S(2)}) async-start(), calls=%async_computation.9 | async-start | bytes 9437184 | tf_op jit(solution)/shard_map/all_gather | solution.py:95
  177.5 584.0 %all-reduce.8.cloned.1.call-start = ((), (), s32[]{:S(2)}) async-start(), calls=%async_computation.10 | async-start | bytes 16777216 | tf_op jit(solution)/shard_map/psum | solution.py:70
  450.6 125.7 %copy-start.49 = (f32[2048]{0:T(1024)S(1)}, f32[2048]{0:T(1024)}, u32[]{:S(2)}) copy-start(f32[2048]{0:T(1024)} %param.35) | copy-start | bytes 24580
  576.3 22.9 %copy-start.55 = (bf16[2048,2048]{1,0:T(8,128)(2,1)S(1)}, bf16[2048,2048]{1,0:T(8,128)(2,1)}, u32[]{:S(2)}) copy-start(bf16[2048,2048]{1,0:T(8,128)(2,1)} %all-gather.9.cloned.1.call-done) | copy-start | bytes 25165828
  610.3 513.0 %all-reduce.10.cloned.1.call-start = ((), (), s32[]{:S(2)}) async-start(), calls=%async_computation.16 | async-start | bytes 33554432 | tf_op jit(solution)/shard_map/psum | solution.py:70
  834.1 289.2 %copy-start.27 = (f32[2048,1]{0,1:T(1,128)S(1)}, f32[2048,1]{0,1:T(1,128)}, u32[]{:S(2)}) copy-start(f32[2048,1]{0,1:T(1,128)} %copy-done.26) | copy-start | bytes 24580
  834.1 289.1 %copy-start.29 = (f32[1024]{0:T(1024)S(1)}, f32[1024]{0:T(1024)}, u32[]{:S(2)}) copy-start(f32[1024]{0:T(1024)} %copy-done.28) | copy-start | bytes 12292
  834.1 403.0 %reduce-scatter.10.cloned.1.call-start = ((), (), s32[]{:S(2)}) async-start(), calls=%async_computation.13 | async-start | bytes 4718592 | tf_op jit(solution)/shard_map/reduce_scatter | solution.py:226
  844.8 284.8 %copy-start.33 = (f32[1024]{0:T(1024)S(1)}, f32[1024]{0:T(1024)}, u32[]{:S(2)}) copy-start(f32[1024]{0:T(1024)} %copy-done.32) | copy-start | bytes 12292
  844.8 284.8 %copy-start.31 = (f32[1024]{0:T(1024)S(1)}, f32[1024]{0:T(1024)}, u32[]{:S(2)}) copy-start(f32[1024]{0:T(1024)} %copy-done.30) | copy-start | bytes 12292
  844.9 436.4 %reduce-scatter.6.cloned.1.call-start = ((), (), s32[]{:S(2)}) async-start(), calls=%async_computation.11 | async-start | bytes 73728 | tf_op jit(solution)/shard_map/reduce_scatter | solution.py:229
  1135.5 11.2 copy-start.17
  1135.5 11.2 copy-start.47
  1146.5 345.5 %reduce-scatter.8.cloned.1.call-start = ((), (), s32[]{:S(2)}) async-start(), calls=%async_computation.12 | async-start | bytes 14155776 | tf_op jit(solution)/shard_map/reduce_scatter | solution.py:225
  1160.3 616.9 %reduce-scatter.12.cloned.1.call-start = ((), (), s32[]{:S(2)}) async-start(), calls=%async_computation.14 | async-start | bytes 18874368 | tf_op jit(solution)/shard_map/reduce_scatter | solution.py:227
  1177.4 885.3 %reduce-scatter.14.cloned.1.call-start = ((), (), s32[]{:S(2)}) async-start(), calls=%async_computation.15 | async-start | bytes 18874368 | tf_op jit(solution)/shard_map/reduce_scatter | solution.py:228
  1194.8 871.9 %copy-start.34 = (f32[2048,1]{0,1:T(1,128)S(1)}, f32[2048,1]{0,1:T(1,128)}, u32[]{:S(2)}) copy-start(f32[2048,1]{0,1:T(1,128)} %get-tuple-element.119) | copy-start | bytes 24580
  2066.7 50.2 %copy-start.50 = (f32[2048]{0:T(1024)S(1)}, f32[2048]{0:T(1024)}, u32[]{:S(2)}) copy-start(f32[2048]{0:T(1024)} %param.42) | copy-start | bytes 24580
  2066.8 51.6 %copy-start.41 = (f32[2,512]{1,0:T(2,128)S(1)}, f32[2,512]{1,0:T(2,128)}, u32[]{:S(2)}) copy-start(f32[2,512]{1,0:T(2,128)} %param.32) | copy-start | bytes 12292
  2066.8 51.6 %copy-start.53 = (f32[2,512]{1,0:T(2,128)S(1)}, f32[2,512]{1,0:T(2,128)}, u32[]{:S(2)}) copy-start(f32[2,512]{1,0:T(2,128)} %param.39) | copy-start | bytes 12292
  2066.8 52.2 %copy-start.52 = (f32[2,512]{1,0:T(2,128)S(1)}, f32[2,512]{1,0:T(2,128)}, u32[]{:S(2)}) copy-start(f32[2,512]{1,0:T(2,128)} %param.46) | copy-start | bytes 12292
  2066.8 52.7 %copy-start.42 = (f32[2048]{0:T(1024)S(1)}, f32[2048]{0:T(1024)}, u32[]{:S(2)}) copy-start(f32[2048]{0:T(1024)} %param.49) | copy-start | bytes 24580
  2066.8 53.3 %copy-start.37 = (f32[256,6]{0,1:T(8,128)S(1)}, f32[256,6]{0,1:T(8,128)}, u32[]{:S(2)}) copy-start(f32[256,6]{0,1:T(8,128)} %param.31) | copy-start | bytes 18436
  2066.8 53.3 %copy-start.38 = (f32[256,6]{0,1:T(8,128)S(1)}, f32[256,6]{0,1:T(8,128)}, u32[]{:S(2)}) copy-start(f32[256,6]{0,1:T(8,128)} %reduce-scatter.6.cloned.1.call-done) | copy-start | bytes 18436
  2066.8 53.3 %copy-start.51 = (f32[256,6]{0,1:T(8,128)S(1)}, f32[256,6]{0,1:T(8,128)}, u32[]{:S(2)}) copy-start(f32[256,6]{0,1:T(8,128)} %param.38) | copy-start | bytes 18436
  2066.8 54.6 %copy-start.43 = (f32[256,6]{0,1:T(8,128)S(1)}, f32[256,6]{0,1:T(8,128)}, u32[]{:S(2)}) copy-start(f32[256,6]{0,1:T(8,128)} %param.45) | copy-start | bytes 18436
  2066.9 60.6 %copy-start.12 = (f32[256,3,512]{2,0,1:T(8,128)S(1)}, f32[256,3,512]{2,0,1:T(8,128)}, u32[]{:S(2)}) copy-start(f32[256,3,512]{2,0,1:T(8,128)} %param.33) | copy-start | bytes 4718596
  2066.9 60.6 %copy-start.13 = (f32[256,3,512]{2,0,1:T(8,128)S(1)}, f32[256,3,512]{2,0,1:T(8,128)}, u32[]{:S(2)}) copy-start(f32[256,3,512]{2,0,1:T(8,128)} %reduce-scatter.8.cloned.1.call-done) | copy-start | bytes 4718596
  2116.9 16.5 copy-start.25
  2118.3 16.7 copy-start.35
  2118.9 16.1 copy-start.39
  2121.4 13.7 copy-start.36
  2125.3 15.0 copy-start.22
  2125.3 9.8 copy-start.11
  2125.3 9.8 copy-start.23
  (23 other events, 132.8 us)
Sparse Core Ops, SparseCore 0:
  10.7 102.9 all-gather.4
  116.4 47.5 all-gather.6
  171.5 151.3 all-reduce.5
  325.5 125.0 all-gather.8
  453.1 123.1 all-gather.10
  610.4 151.0 all-reduce.7
  834.2 288.9 all-reduce.9
  1127.5 88.2 reduce-scatter.9
  1220.1 61.1 reduce-scatter.5
  1285.1 206.7 reduce-scatter.7
  1496.2 280.9 reduce-scatter.11
  1780.9 281.7 reduce-scatter.13
where the time goes:
time: 2160 us; the launch traced here: 2150 us
  waiting for transfers between devices  1660 us (77%)
  matrix products  195 us (9%)
  other arithmetic  128 us (6%)
  blocking collectives  128 us (6%)
  between operations  23.6 us (1%)
    psum x3, waiting for transfers between devices, sum_over_mp(): summed = lax.psum(term_fn(0, row_count), 'mp')  533 us
    reduce_scatter x1, waiting for transfers between devices, local(): lax.psum_scatter(down_sum, 'dp', scatter_dimension=0, tiled=True)  281 us
    reduce_scatter x1, waiting for transfers between devices, local(): lax.psum_scatter(fc_sum, 'dp', scatter_dimension=0, tiled=True)  281 us
    reduce_scatter x1, waiting for transfers between devices, local(): lax.psum_scatter(qkv_sum, 'dp', scatter_dimension=0, tiled=True)  208 us
    all_gather x1, waiting for transfers between devices, local(): lax.all_gather(low_fc, 'dp', axis=0, tiled=True)  118 us
    all_gather x1, waiting for transfers between devices, local(): lax.all_gather(low_down, 'dp', axis=0, tiled=True)  110 us
    all_gather x1, waiting for transfers between devices, local(): lax.all_gather(low_qkv, 'dp', axis=0, tiled=True)  61 us
  transfers between devices with their start and end apart: 12, of which 11 were waited for; matrix products, arithmetic and copies ran while one was open for 8% of the time, Pallas kernels for 0%

commit v1 on v0

--- a/solution.py
+++ b/solution.py
@@ -11,6 +11,27 @@
 RATE = 192.0
 KEEP = 0.9
 NEG = -1e30
+
+
+def ring_gather(x, axis, dim):
+    devices, place, extent = (lax.axis_size(axis), lax.axis_index(axis), x.shape[dim])
+    upward = [(i, (i + 1) % devices) for i in range(devices)]
+    left = [(i, (i - 1) % devices) for i in range(devices)]
+    filled = jnp.zeros((*x.shape[:dim], devices * extent, *x.shape[dim + 1 :]), x.dtype)
+    filled = lax.dynamic_update_slice_in_dim(filled, x, place * extent, axis=dim)
+    from_left = from_right = x
+    half = devices // 2
+    for step in range(1, half + 1):
+        from_left = lax.ppermute(from_left, axis, upward)
+        filled = lax.dynamic_update_slice_in_dim(
+            filled, from_left, (place - step) % devices * extent, axis=dim
+        )
+        if step < devices - half:
+            from_right = lax.ppermute(from_right, axis, left)
+            filled = lax.dynamic_update_slice_in_dim(
+                filled, from_right, (place + step) % devices * extent, axis=dim
+            )
+    return filled
 
 
 def layer_norm(value, gain, shift):
@@ -91,7 +112,7 @@
     w_qkv, w_proj, w_fc, w_down, w_norm = (
         lax.all_gather(low_qkv, "dp", axis=0, tiled=True),
         lax.all_gather(low_proj, "dp", axis=0, tiled=True),
-        lax.all_gather(low_fc, "dp", axis=0, tiled=True),
+        ring_gather(low_fc, "dp", 0),
         lax.all_gather(low_down, "dp", axis=0, tiled=True),
         lax.all_gather(low_norm, "dp", axis=0, tiled=True),
     )

time: 2160 us -> 2040 us (0.944)
  waiting for transfers between devices: 1660 us -> 1480 us
  blocking collectives: 128 us -> 166 us
    psum x3, waiting for transfers between devices: 533 us -> 411 us  [sum_over_mp(): summed = lax.psum(term_fn(0, row_count), 'mp')]
    all_gather x1 -> x0, waiting for transfers between devices: 118 us -> none  [local(): lax.all_gather(low_fc, 'dp', axis=0, tiled=True)]
    ppermute x0 -> x7, waiting for transfers between devices: none -> 105 us  [the longest x4 61.5 us: ring_gather(): from_left = lax.ppermute(from_left, axis, upward)]
    all_gather x1, waiting for transfers between devices: 110 us -> 63.2 us  [local(): lax.all_gather(low_down, 'dp', axis=0, tiled=True)]
    psum x1, blocking collectives: 18.5 us -> 55.8 us  [local(): counts = lax.psum(local_counts, 'dp')]
  transfers between devices with their start and end apart: 12 -> 18, of which waited for: 11 -> 13; matrix products, arithmetic and copies ran while one was open for 8% -> 9% of each run, Pallas kernels for 0% -> 0%
where the time goes in v1:
time: 2040 us
  waiting for transfers between devices  1480 us (73%)
  matrix products  194 us (10%)
  blocking collectives  166 us (8%)
  other arithmetic  128 us (6%)
  local copies, waits for them, and re-layouts  34.5 us (2%)
  between operations  23.5 us (1%)
    psum x3, waiting for transfers between devices, sum_over_mp(): summed = lax.psum(term_fn(0, row_count), 'mp')  411 us
    reduce_scatter x1, waiting for transfers between devices, local(): lax.psum_scatter(fc_sum, 'dp', scatter_dimension=0, tiled=True)  282 us
    reduce_scatter x1, waiting for transfers between devices, local(): lax.psum_scatter(down_sum, 'dp', scatter_dimension=0, tiled=True)  282 us
    reduce_scatter x1, waiting for transfers between devices, local(): lax.psum_scatter(qkv_sum, 'dp', scatter_dimension=0, tiled=True)  208 us
    all_gather x1, waiting for transfers between devices, local(): lax.all_gather(low_down, 'dp', axis=0, tiled=True)  63.2 us
    ppermute x4, waiting for transfers between devices, ring_gather(): from_left = lax.ppermute(from_left, axis, upward)  61.5 us
    all_gather x1, waiting for transfers between devices, local(): lax.all_gather(low_qkv, 'dp', axis=0, tiled=True)  61 us
    psum x1, blocking collectives, local(): counts = lax.psum(local_counts, 'dp')  55.8 us
  transfers between devices with their start and end apart: 18, of which 13 were waited for; matrix products, arithmetic and copies ran while one was open for 9% of the time, Pallas kernels for 0%

profile of v1, /device:TPU:0, one launch (start us, length us, event | category | flops | bytes accessed | tf_op | source)
XLA Modules:
  0.0 2035.3 jit_solution(15516491576927316506)
XLA Ops:
  15.6 3.4 fusion.15
  19.1 32.9 %all_gather.12 = bf16[2048,6]{0,1:T(8,128)(2,1)S(1)} all-gather(bf16[256,6]{0,1:T(8,128)(2,1)S(1)} %convert_element_type.108), channel_id=1, replica_groups=mesh['dp'=8,'mp'=4] {'dp'}, dimensions={0}, use_global_device_ids=true | all-gather | bytes 27648 | tf_op jit(solution)/shard_map/all_gather | solution.py:117
  52.7 61.0 %all-gather.4.cloned.1.call-done = bf16[2048,3,512]{0,2,1:T(8,128)(2,1)} async-done(((bf16[256,3,512]{0,2,1:T(8,128)(2,1)}), bf16[2048,3,512]{0,2,1:T(8,128)(2,1)}) %all-gather.4.cloned.1.call-update) | async-done | bytes 6291472 | tf_op jit(solution)/shard_map/all_gather | solution.py:113
  113.7 11.1 add_convert_fusion.2
  124.9 3.3 fusion
  128.3 3.7 exponential_reduce_fusion
  134.0 6.5 convolution_convert_fusion.1
  140.4 23.5 %all-gather.6.cloned.1.call-done = bf16[2048,512]{1,0:T(8,128)(2,1)} async-done(((bf16[256,512]{1,0:T(8,128)(2,1)}), bf16[2048,512]{1,0:T(8,128)(2,1)}) %all-gather.6.cloned.1.call-update) | async-done | bytes 2097168 | tf_op jit(solution)/shard_map/all_gather | solution.py:114
  163.9 7.4 fusion.66
  174.2 4.3 broadcast_in_dim.107
  182.1 3.8 collective-permute-start.1
  185.9 40.0 %collective-permute-done = bf16[256,2048]{1,0:T(8,128)(2,1)S(1)} collective-permute-done((bf16[256,2048]{1,0:T(8,128)(2,1)S(1)}, bf16[256,2048]{1,0:T(8,128)(2,1)S(1)}, u32[]{:S(2)}, u32[]{:S(2)}) %collective-permute-start) | collective-permute-done | bytes 1048608 | tf_op jit(solution)/shard_map/ppermute | solution.py:25
  231.6 21.5 %collective-permute-done.2 = bf16[256,2048]{1,0:T(8,128)(2,1)} collective-permute-done((bf16[256,2048]{1,0:T(8,128)(2,1)S(1)}, bf16[256,2048]{1,0:T(8,128)(2,1)}, u32[]{:S(2)}, u32[]{:S(2)}) %collective-permute-start.2) | collective-permute-done | bytes 1048608 | tf_op jit(solution)/shard_map/ppermute | solution.py:25
  254.4 55.8 %psum.58 = f32[4]{0:T(128)S(1)} all-reduce(f32[4]{0:T(128)S(1)} %fusion.44), channel_id=1, replica_groups=mesh['dp'=8,'mp'=4] {'dp'}, use_global_device_ids=true, to_apply=%region_9.10 | all-reduce | flops 4 | bytes 32 | tf_op jit(solution)/shard_map/psum | solution.py:97
  326.5 42.6 %collective-permute-done.5 = bf16[256,2048]{1,0:T(8,128)(2,1)S(1)} collective-permute-done((bf16[256,2048]{1,0:T(8,128)(2,1)}, bf16[256,2048]{1,0:T(8,128)(2,1)S(1)}, u32[]{:S(2)}, u32[]{:S(2)}) %collective-permute-start.5) | collective-permute-done | bytes 1048608 | tf_op jit(solution)/shard_map/ppermute | solution.py:30
  371.2 5.8 fusion.62
  380.3 13.7 fusion.51
  393.9 63.2 %all-gather.8.cloned.1.call-done = bf16[2048,2048]{1,0:T(8,128)(2,1)} async-done(((bf16[256,2048]{1,0:T(8,128)(2,1)}), bf16[2048,2048]{1,0:T(8,128)(2,1)}) %all-gather.8.cloned.1.call-update) | async-done | bytes 8388624 | tf_op jit(solution)/shard_map/all_gather | solution.py:116
  457.1 20.4 %convert_reduce_fusion.1 = (f32[2048]{0:T(1024)}, bf16[1024,2048]{1,0:T(8,128)(2,1)S(1)}) fusion(bf16[2048,2048]{1,0:T(8,128)(2,1)} %all-gather.8.cloned.1.call-done, bf16[1024,2048]{1,0:T(8,128)(2,1)} %param.27, f32[1024]{0:T(1024)S(1)} %fusion.41, f32[1024,2048]{1,0:T(8,128)} %fusion.51, f32[2048]{0:T(1024)S(1)} %copy-done.50), kind=kOutput, calls=%fused_computation.34 | convolution fusion | flops 8652847104 | bytes 25186304 | tf_op jit(solution)/shard_map/td,df->tf/dot_general | solution.py:172
  479.5 13.2 fusion.67
  492.7 18.3 fusion.49
  511.0 132.9 %all-reduce.8.cloned.1.call-done = f32[1024,2048]{1,0:T(8,128)} async-done(((f32[1024,2048]{1,0:T(8,128)}), f32[1024,2048]{1,0:T(8,128)}) %all-reduce.8.cloned.1.call-update) | async-done | bytes 8388624 | tf_op jit(solution)/shard_map/psum | solution.py:91
  643.9 7.5 multiply_reduce_fusion.1
  652.1 5.0 fusion.61
  657.1 6.3 fusion.33
  663.5 9.7 convolution_convert_fusion
  673.1 12.6 multiply_reduce_fusion
  685.7 12.1 multiply_convert_fusion
  705.5 11.0 convolution_bitcast_fusion
  717.8 9.5 fusion.23
  727.3 278.3 %all-reduce.10.cloned.1.call-done = (f32[1024,2048]{1,0:T(8,128)}, f32[1024,2048]{1,0:T(8,128)}) async-done(((f32[1024,2048]{1,0:T(8,128)}, f32[1024,2048]{1,0:T(8,128)}), (f32[1024,2048]{1,0:T(8,128)}, f32[1024,2048]{1,0:T(8,128)})) %all-reduce.10.cloned.1.call-update) | async-done | bytes 16777232 | tf_op jit(solution)/shard_map/psum | solution.py:91
  1005.7 6.3 fusion.53
  1014.0 3.9 fusion.10
  1018.0 10.2 fusion.20
  1029.2 13.6 fusion.36
  1043.4 16.4 fusion.50
  1060.1 17.1 fusion.27
  1077.9 37.8 %all-reduce = (f32[2,512]{1,0:T(2,128)S(1)}, f32[2048]{0:T(1024)S(1)}) all-reduce(f32[2,512]{1,0:T(2,128)S(1)} %convert_reduce_fusion.2, f32[2048]{0:T(1024)S(1)} %copy-done.49), channel_id=1, replica_groups=mesh['dp'=8,'mp'=4] {'dp'}, use_global_device_ids=true, to_apply=%region_28.29 | all-reduce | flops 3072 | bytes 24576 | tf_op jit(solution)/shard_map/psum | solution.py:252
  1122.0 41.7 %reduce-scatter.6.cloned.1.call-done = f32[256,6]{0,1:T(8,128)} async-done(((f32[2048,6]{0,1:T(8,128)}), f32[256,6]{0,1:T(8,128)}) %reduce-scatter.6.cloned.1.call-update) | async-done | bytes 6160 | tf_op jit(solution)/shard_map/reduce_scatter | solution.py:250
  1166.3 208.2 %reduce-scatter.8.cloned.1.call-done = f32[256,3,512]{2,0,1:T(8,128)} async-done(((f32[2048,3,512]{2,0,1:T(8,128)}), f32[256,3,512]{2,0,1:T(8,128)}) %reduce-scatter.8.cloned.1.call-update) | async-done | bytes 1572880 | tf_op jit(solution)/shard_map/reduce_scatter | solution.py:246
  1378.9 281.6 %reduce-scatter.12.cloned.1.call-done = f32[256,2048]{1,0:T(8,128)} async-done(((f32[2048,2048]{1,0:T(8,128)}), f32[256,2048]{1,0:T(8,128)}) %reduce-scatter.12.cloned.1.call-update) | async-done | bytes 2097168 | tf_op jit(solution)/shard_map/reduce_scatter | solution.py:248
  1660.5 3.4 multiply_reduce_fusion.5
  1664.5 281.6 %reduce-scatter.14.cloned.1.call-done = f32[256,2048]{1,0:T(8,128)} async-done(((f32[2048,2048]{1,0:T(8,128)}), f32[256,2048]{1,0:T(8,128)}) %reduce-scatter.14.cloned.1.call-update) | async-done | bytes 2097168 | tf_op jit(solution)/shard_map/reduce_scatter | solution.py:249
  1946.1 3.4 multiply_reduce_fusion.4
  1950.3 10.2 add_convert_fusion
  1960.4 39.2 %psum.63 = f32[]{:T(128)} all-reduce(f32[]{:T(128)S(6)} %add.326), channel_id=1, replica_groups=mesh['dp'=8,'mp'=4] {'dp','mp'}, use_global_device_ids=true, to_apply=%region_41.42 | all-reduce | flops 1 | bytes 8 | tf_op jit(solution)/shard_map/psum | solution.py:270
  2010.9 5.9 fusion.58
  2018.5 5.1 fusion.54
  (209 shorter events, 86.4 us)
Async XLA Ops:
  7.2 106.5 %all-gather.4.cloned.1.call-start = ((), (), s32[]{:S(2)}) async-start(), calls=%async_computation.5 | async-start | bytes 7077888 | tf_op jit(solution)/shard_map/all_gather | solution.py:113
  9.9 154.0 %all-gather.6.cloned.1.call-start = ((), (), s32[]{:S(2)}) async-start(), calls=%async_computation.6 | async-start | bytes 2359296 | tf_op jit(solution)/shard_map/all_gather | solution.py:114
  11.7 359.5 %all-reduce.6.cloned.1.call-start = ((), (), s32[]{:S(2)}) async-start(), calls=%async_computation.7 | async-start | bytes 16777216 | tf_op jit(solution)/shard_map/psum | solution.py:91
  15.6 109.2 %copy-start.29 = (f32[1024]{0:T(1024)}, f32[1024]{0:T(1024)S(1)}, u32[]{:S(2)}) copy-start(f32[1024]{0:T(1024)S(1)} %broadcast_multiply_fusion.8) | copy-start | bytes 12292
  19.0 105.8 %copy-start.33 = (f32[1024]{0:T(1024)}, f32[1024]{0:T(1024)S(1)}, u32[]{:S(2)}) copy-start(f32[1024]{0:T(1024)S(1)} %fusion.15) | copy-start | bytes 12292
  19.1 105.8 %copy-start.31 = (f32[1024]{0:T(1024)}, f32[1024]{0:T(1024)S(1)}, u32[]{:S(2)}) copy-start(f32[1024]{0:T(1024)S(1)} %fusion.42) | copy-start | bytes 12292
  52.6 72.3 %copy-start.27 = (f32[2048,1]{0,1:T(1,128)}, f32[2048,1]{0,1:T(1,128)S(1)}, u32[]{:S(2)}) copy-start(f32[2048,1]{0,1:T(1,128)S(1)} %get-tuple-element.125) | copy-start | bytes 24580
  52.6 72.3 %copy-start.47 = (f32[2048,1]{0,1:T(1,128)}, f32[2048,1]{0,1:T(1,128)S(1)}, u32[]{:S(2)}) copy-start(f32[2048,1]{0,1:T(1,128)S(1)} %get-tuple-element.126) | copy-start | bytes 24580
  52.6 325.4 %copy-start.45 = (f32[2048,1]{0,1:T(1,128)}, f32[2048,1]{0,1:T(1,128)S(1)}, u32[]{:S(2)}) copy-start(f32[2048,1]{0,1:T(1,128)S(1)} %get-tuple-element.123) | copy-start | bytes 24580
  140.4 30.9 %copy-start.56 = (bf16[4,128,1024]{2,1,0:T(8,128)(2,1)}, bf16[4,128,1024]{2,1,0:T(8,128)(2,1)S(1)}, u32[]{:S(2)}) copy-start(bf16[4,128,1024]{2,1,0:T(8,128)(2,1)S(1)} %convolution_convert_fusion.1) | copy-start | bytes 3145732
  171.3 139.0 %copy-start.55 = (s32[4]{0:T(128)S(1)}, s32[4]{0:T(128)}, u32[]{:S(2)}) copy-start(s32[4]{0:T(128)} %param.30) | copy-start | bytes 52
  171.3 285.8 %all-gather.8.cloned.1.call-start = ((), (), s32[]{:S(2)}) async-start(), calls=%async_computation.8 | async-start | bytes 9437184 | tf_op jit(solution)/shard_map/all_gather | solution.py:116
  174.1 469.7 %all-reduce.8.cloned.1.call-start = ((), (), s32[]{:S(2)}) async-start(), calls=%async_computation.9 | async-start | bytes 16777216 | tf_op jit(solution)/shard_map/psum | solution.py:91
  181.2 44.7 %collective-permute-start = (bf16[256,2048]{1,0:T(8,128)(2,1)S(1)}, bf16[256,2048]{1,0:T(8,128)(2,1)S(1)}, u32[]{:S(2)}, u32[]{:S(2)}) collective-permute-start(bf16[256,2048]{1,0:T(8,128)(2,1)S(1)} %get-tuple-element.119), channel_id=1, source_target_pairs={{0,4},{4,8},{8,12},{12,16},{16,20},{20,24},{24,28},{28,0},{1,5},{5... | collective-permute-start | bytes 3145736 | tf_op jit(solution)/shard_map/ppermute | solution.py:25
  182.1 46.9 %collective-permute-start.1 = (bf16[256,2048]{1,0:T(8,128)(2,1)S(1)}, bf16[256,2048]{1,0:T(8,128)(2,1)S(1)}, u32[]{:S(2)}, u32[]{:S(2)}) collective-permute-start(bf16[256,2048]{1,0:T(8,128)(2,1)S(1)} %get-tuple-element.119), channel_id=1, source_target_pairs={{0,28},{4,0},{8,4},{12,8},{16,12},{20,16},{24,20},{28,24},{1,29},{... | collective-permute-start | bytes 3145736 | tf_op jit(solution)/shard_map/ppermute | solution.py:30
  225.9 27.1 %collective-permute-start.2 = (bf16[256,2048]{1,0:T(8,128)(2,1)S(1)}, bf16[256,2048]{1,0:T(8,128)(2,1)}, u32[]{:S(2)}, u32[]{:S(2)}) collective-permute-start(bf16[256,2048]{1,0:T(8,128)(2,1)S(1)} %collective-permute-done), channel_id=1, source_target_pairs={{0,4},{4,8},{8,12},{12,16},{16,20},{20,24},{24,28},{28,0},{1,5},{5... | collective-permute-start | bytes 3145736 | tf_op jit(solution)/shard_map/ppermute | solution.py:25
  229.0 85.1 %collective-permute-start.3 = (bf16[256,2048]{1,0:T(8,128)(2,1)S(1)}, bf16[256,2048]{1,0:T(8,128)(2,1)}, u32[]{:S(2)}, u32[]{:S(2)}) collective-permute-start(bf16[256,2048]{1,0:T(8,128)(2,1)S(1)} %collective-permute-done.1), channel_id=1, source_target_pairs={{0,28},{4,0},{8,4},{12,8},{16,12},{20,16},{24,20},{28,24},{1,29},{... | collective-permute-start | bytes 3145736 | tf_op jit(solution)/shard_map/ppermute | solution.py:30
  253.0 63.7 %collective-permute-start.4 = (bf16[256,2048]{1,0:T(8,128)(2,1)}, bf16[256,2048]{1,0:T(8,128)(2,1)}, u32[]{:S(2)}, u32[]{:S(2)}) collective-permute-start(bf16[256,2048]{1,0:T(8,128)(2,1)} %collective-permute-done.2), channel_id=1, source_target_pairs={{0,4},{4,8},{8,12},{12,16},{16,20},{20,24},{24,28},{28,0},{1,5},{5... | collective-permute-start | bytes 3145736 | tf_op jit(solution)/shard_map/ppermute | solution.py:25
  314.1 55.0 %collective-permute-start.5 = (bf16[256,2048]{1,0:T(8,128)(2,1)}, bf16[256,2048]{1,0:T(8,128)(2,1)S(1)}, u32[]{:S(2)}, u32[]{:S(2)}) collective-permute-start(bf16[256,2048]{1,0:T(8,128)(2,1)} %collective-permute-done.3), channel_id=1, source_target_pairs={{0,28},{4,0},{8,4},{12,8},{16,12},{20,16},{24,20},{28,24},{1,29},{... | collective-permute-start | bytes 3145736 | tf_op jit(solution)/shard_map/ppermute | solution.py:30
  316.7 53.5 %collective-permute-start.6 = (bf16[256,2048]{1,0:T(8,128)(2,1)}, bf16[256,2048]{1,0:T(8,128)(2,1)S(1)}, u32[]{:S(2)}, u32[]{:S(2)}) collective-permute-start(bf16[256,2048]{1,0:T(8,128)(2,1)} %collective-permute-done.4), channel_id=1, source_target_pairs={{0,4},{4,8},{8,12},{12,16},{16,20},{20,24},{24,28},{28,0},{1,5},{5... | collective-permute-start | bytes 3145736 | tf_op jit(solution)/shard_map/ppermute | solution.py:25
  380.3 76.8 %copy-start.50 = (f32[2048]{0:T(1024)S(1)}, f32[2048]{0:T(1024)}, u32[]{:S(2)}) copy-start(f32[2048]{0:T(1024)} %param.35) | copy-start | bytes 24580
  492.7 513.0 %all-reduce.10.cloned.1.call-start = ((), (), s32[]{:S(2)}) async-start(), calls=%async_computation.15 | async-start | bytes 33554432 | tf_op jit(solution)/shard_map/psum | solution.py:91
  716.6 289.2 %copy-start.28 = (f32[2048,1]{0,1:T(1,128)S(1)}, f32[2048,1]{0,1:T(1,128)}, u32[]{:S(2)}) copy-start(f32[2048,1]{0,1:T(1,128)} %copy-done.27) | copy-start | bytes 24580
  716.6 289.1 %copy-start.30 = (f32[1024]{0:T(1024)S(1)}, f32[1024]{0:T(1024)}, u32[]{:S(2)}) copy-start(f32[1024]{0:T(1024)} %copy-done.29) | copy-start | bytes 12292
  716.6 403.0 %reduce-scatter.10.cloned.1.call-start = ((), (), s32[]{:S(2)}) async-start(), calls=%async_computation.12 | async-start | bytes 4718592 | tf_op jit(solution)/shard_map/reduce_scatter | solution.py:247
  727.3 284.8 %copy-start.34 = (f32[1024]{0:T(1024)S(1)}, f32[1024]{0:T(1024)}, u32[]{:S(2)}) copy-start(f32[1024]{0:T(1024)} %copy-done.33) | copy-start | bytes 12292
  727.3 284.8 %copy-start.32 = (f32[1024]{0:T(1024)S(1)}, f32[1024]{0:T(1024)}, u32[]{:S(2)}) copy-start(f32[1024]{0:T(1024)} %copy-done.31) | copy-start | bytes 12292
  727.3 436.4 %reduce-scatter.6.cloned.1.call-start = ((), (), s32[]{:S(2)}) async-start(), calls=%async_computation.10 | async-start | bytes 73728 | tf_op jit(solution)/shard_map/reduce_scatter | solution.py:250
  1028.9 345.6 %reduce-scatter.8.cloned.1.call-start = ((), (), s32[]{:S(2)}) async-start(), calls=%async_computation.11 | async-start | bytes 14155776 | tf_op jit(solution)/shard_map/reduce_scatter | solution.py:246
  1042.8 617.7 %reduce-scatter.12.cloned.1.call-start = ((), (), s32[]{:S(2)}) async-start(), calls=%async_computation.13 | async-start | bytes 18874368 | tf_op jit(solution)/shard_map/reduce_scatter | solution.py:248
  1059.9 886.2 %reduce-scatter.14.cloned.1.call-start = ((), (), s32[]{:S(2)}) async-start(), calls=%async_computation.14 | async-start | bytes 18874368 | tf_op jit(solution)/shard_map/reduce_scatter | solution.py:249
  1077.2 872.9 %copy-start.35 = (f32[2048,1]{0,1:T(1,128)S(1)}, f32[2048,1]{0,1:T(1,128)}, u32[]{:S(2)}) copy-start(f32[2048,1]{0,1:T(1,128)} %get-tuple-element.121) | copy-start | bytes 24580
  1950.1 50.2 %copy-start.51 = (f32[2048]{0:T(1024)S(1)}, f32[2048]{0:T(1024)}, u32[]{:S(2)}) copy-start(f32[2048]{0:T(1024)} %param.42) | copy-start | bytes 24580
  1950.1 51.6 %copy-start.42 = (f32[2,512]{1,0:T(2,128)S(1)}, f32[2,512]{1,0:T(2,128)}, u32[]{:S(2)}) copy-start(f32[2,512]{1,0:T(2,128)} %param.32) | copy-start | bytes 12292
  1950.2 51.6 %copy-start.54 = (f32[2,512]{1,0:T(2,128)S(1)}, f32[2,512]{1,0:T(2,128)}, u32[]{:S(2)}) copy-start(f32[2,512]{1,0:T(2,128)} %param.39) | copy-start | bytes 12292
  1950.2 52.2 %copy-start.53 = (f32[2,512]{1,0:T(2,128)S(1)}, f32[2,512]{1,0:T(2,128)}, u32[]{:S(2)}) copy-start(f32[2,512]{1,0:T(2,128)} %param.46) | copy-start | bytes 12292
  1950.2 52.7 %copy-start.43 = (f32[2048]{0:T(1024)S(1)}, f32[2048]{0:T(1024)}, u32[]{:S(2)}) copy-start(f32[2048]{0:T(1024)} %param.49) | copy-start | bytes 24580
  1950.2 53.3 %copy-start.38 = (f32[256,6]{0,1:T(8,128)S(1)}, f32[256,6]{0,1:T(8,128)}, u32[]{:S(2)}) copy-start(f32[256,6]{0,1:T(8,128)} %param.31) | copy-start | bytes 18436
  1950.2 53.3 %copy-start.39 = (f32[256,6]{0,1:T(8,128)S(1)}, f32[256,6]{0,1:T(8,128)}, u32[]{:S(2)}) copy-start(f32[256,6]{0,1:T(8,128)} %reduce-scatter.6.cloned.1.call-done) | copy-start | bytes 18436
  1950.2 53.3 %copy-start.52 = (f32[256,6]{0,1:T(8,128)S(1)}, f32[256,6]{0,1:T(8,128)}, u32[]{:S(2)}) copy-start(f32[256,6]{0,1:T(8,128)} %param.38) | copy-start | bytes 18436
  1950.2 54.6 %copy-start.44 = (f32[256,6]{0,1:T(8,128)S(1)}, f32[256,6]{0,1:T(8,128)}, u32[]{:S(2)}) copy-start(f32[256,6]{0,1:T(8,128)} %param.45) | copy-start | bytes 18436
  1950.2 60.6 %copy-start.12 = (f32[256,3,512]{2,0,1:T(8,128)S(1)}, f32[256,3,512]{2,0,1:T(8,128)}, u32[]{:S(2)}) copy-start(f32[256,3,512]{2,0,1:T(8,128)} %param.33) | copy-start | bytes 4718596
  1950.3 60.6 %copy-start.13 = (f32[256,3,512]{2,0,1:T(8,128)S(1)}, f32[256,3,512]{2,0,1:T(8,128)}, u32[]{:S(2)}) copy-start(f32[256,3,512]{2,0,1:T(8,128)} %reduce-scatter.8.cloned.1.call-done) | copy-start | bytes 4718596
  2000.3 16.5 copy-start.25
  2001.7 16.7 copy-start.36
  2002.3 16.1 copy-start.40
  2004.8 13.7 copy-start.37
  2008.6 15.0 copy-start.22
  (29 other events, 189.8 us)
Sparse Core Ops, SparseCore 0:
  10.7 102.9 all-gather.3
  116.4 47.4 all-gather.5
  171.4 151.3 all-reduce.5
  325.4 131.6 all-gather.7
  492.8 151.0 all-reduce.7
  716.7 288.9 all-reduce.9
  1009.9 88.2 reduce-scatter.9
  1102.5 61.1 reduce-scatter.5
  1167.8 206.6 reduce-scatter.7
  1378.6 281.8 reduce-scatter.11
  1664.3 281.7 reduce-scatter.13
